TPU v7x, 128 devices: a whole 4x4x4 slice. The times are simulated.
128 devices in a mesh: mem: 8 (over y_hi, x), dom: 16 (over z, y_lo, core).
Axes of the slice: x: 4, y: 4 (y_hi: 2, y_lo: 2; y = y_hi * 2 + y_lo), z: 4, core: 2. Of those that a mesh axis runs over, the one named last changes fastest.
Arguments:
- sample_vectors_prior: float32 [32, 5, 512, 256], P('mem', None, 'dom'), may hold values from -6 to 6
- smoothing_number: float32 [5, 512, 256], P(None, 'dom'), may hold values from 0.02 to 0.2
- cross_quantity_factor: float32 [5, 5], replicated, may hold values from -0.6 to 0.6
- obs_tile: int32 [2, 2048, 1], replicated, may hold values from 0 to 15; in each aligned block of 2048 rows (0 to 2047, 2048 to 4095, ..., all dimensions but the last counted through in order) at most 256 rows name the same one
- measured_gridpoint: int32 [2, 2048], replicated, may hold values from 0 to 7904
- obs_field: int32 [2, 2048], replicated, may hold values from 0 to 4
- obs_weights: float32 [2, 2048, 4], replicated, may hold values from 0.1 to 0.5
- obs_values: float32 [2, 2048], replicated, may hold values from -8 to 8
- observation_variance: float32 [2, 2048], replicated, may hold values from 0.2 to 2
- localization: float32 [2, 16, 2048], P(None, 'dom'), may hold values from 0.001 to 0.02
Outputs:
- analysis: float32 [32, 5, 512, 256], P('mem', None, 'dom')
Inputs may be any that keep to these rules, and one draw needn't show every extreme that they name: `obs_tile`: in each batch at most 256 observations share an owning tile, and in some batch some tile owns exactly 256. Local row measured_gridpoint // 255, column measured_gridpoint % 255; the four points used lie in the owning tile.
All inputs are finite; a program needn't handle non-finite values.
Results may differ from a plain program's by a relative error of at most 0.0001.
Values sent between devices are 32-bit elements; how exact they have to be, the bound alone decides.
No kernel may reach another device: no remote copies, remote signals or barrier semaphores. Data moves between devices by JAX's collectives and lax.ppermute only.
A program may use at most 128 MiB of HBM per device.

v0:
```python
import jax
import jax.numpy as jnp
from jax import lax
from jax.sharding import PartitionSpec as P

STEPS = 2


def with_halo(cells, sides, width):
    for axis, dim in sides:
        count = lax.axis_size(axis)
        ends = count - 1
        head = lax.slice_in_dim(cells, 0, width, axis=dim)
        tail = lax.slice_in_dim(cells, cells.shape[dim] - width, cells.shape[dim], axis=dim)
        cells = jnp.concatenate(
            [
                lax.ppermute(tail, axis, [(i, (i + 1) % count) for i in range(ends)]),
                cells,
                lax.ppermute(head, axis, [((i + 1) % count, i) for i in range(ends)]),
            ],
            axis=dim,
        )
    return cells


def predicted_quantity(sample_vectors_prior, smoothing_number, cross_quantity_factor):
    padded = with_halo(sample_vectors_prior, (("dom", 2),), 1)
    padded = jnp.pad(padded, ((0, 0), (0, 0), (0, 0), (1, 1)))
    lap = padded[:, :, 2:, 1:-1] + padded[:, :, :-2, 1:-1]
    lap = lap + padded[:, :, 1:-1, 2:] + padded[:, :, 1:-1, :-2] - 4.0 * sample_vectors_prior
    mixed = jnp.einsum(
        "fg,mgxy->mfxy",
        cross_quantity_factor,
        sample_vectors_prior,
        precision=lax.Precision.HIGHEST,
    )
    return sample_vectors_prior + smoothing_number[None] * lap + mixed


def local_priors(
    sample_vectors_prior, obs_tile, measured_gridpoint, obs_field, obs_weights, batch_index, my_tile
):
    sample_total_size, fields, tile_row_count, columns = sample_vectors_prior.shape
    nobs_count = measured_gridpoint.shape[1]
    offsets = jnp.array([0, 1, columns, columns + 1], dtype=jnp.int32)
    owner = obs_tile[batch_index, :, 0]
    place = measured_gridpoint[batch_index]
    base = (
        obs_field[batch_index] * (tile_row_count * columns)
        + place // (columns - 1) * columns
        + place % (columns - 1)
    )
    points = (base[:, None] + offsets[None, :]).reshape(-1)
    flat = sample_vectors_prior.reshape(sample_total_size, fields * tile_row_count * columns)
    values = jnp.take(flat, points, axis=1).reshape(sample_total_size, nobs_count, 4)
    local_prior = jnp.sum(values * obs_weights[batch_index][None], axis=-1)
    owned_mask = owner == my_tile
    return (local_prior, owner, owned_mask)


def share_priors(local_prior, owned_mask):
    masked = jnp.where(owned_mask[None], local_prior, jnp.float32(0.0))
    summed = lax.psum(masked, "dom")
    prior = lax.all_gather(summed, "mem", axis=0, tiled=True)
    return prior


def batch_mixing(prior, obs_values, observation_variance, localization, batch_index):
    members = prior.shape[0]
    mean_prior = jnp.mean(prior, axis=0)
    ensemble_spread = prior - mean_prior[None]
    variance = jnp.sum(ensemble_spread * ensemble_spread, axis=0) / (members - 1)
    error = observation_variance[batch_index]
    total = variance + error
    gain = (obs_values[batch_index] - mean_prior)[None] / total[None] - ensemble_spread / (
        jnp.sqrt(total) * (jnp.sqrt(error) + jnp.sqrt(total))
    )[None]
    return jnp.einsum(
        "mo,to,no->tmn",
        ensemble_spread,
        localization[batch_index],
        gain,
        precision=lax.Precision.HIGHEST,
    )[0] / (members - 1)


def apply_update(sample_vectors_prior, mixing):
    sample_total_size, fields, tile_row_count, columns = sample_vectors_prior.shape
    members = sample_total_size * lax.axis_size("mem")
    flat = sample_vectors_prior.reshape(sample_total_size, fields * tile_row_count * columns)
    own_columns = lax.dynamic_slice_in_dim(
        mixing, lax.axis_index("mem") * sample_total_size, sample_total_size, 1
    )
    piece = lax.all_gather(flat, "mem", axis=0, tiled=True)
    product = jnp.dot(
        own_columns.T, piece, precision=lax.Precision.HIGHEST, preferred_element_type=jnp.float32
    )
    member_total = jnp.sum(piece, axis=0)
    average = member_total / members
    updated = flat + product - jnp.sum(own_columns, axis=0)[:, None] * average[None]
    return updated.reshape(sample_total_size, fields, tile_row_count, columns)


def on_device(
    sample_vectors_prior,
    smoothing_number,
    cross_quantity_factor,
    obs_tile,
    measured_gridpoint,
    obs_field,
    obs_weights,
    obs_values,
    observation_variance,
    localization,
):
    my_tile = lax.axis_index("dom")
    for step_index in range(STEPS):
        sample_vectors_prior = predicted_quantity(
            sample_vectors_prior, smoothing_number, cross_quantity_factor
        )
    batch_count = obs_values.shape[0]
    for batch_index in range(batch_count):
        local_prior, owner, owned_mask = local_priors(
            sample_vectors_prior,
            obs_tile,
            measured_gridpoint,
            obs_field,
            obs_weights,
            batch_index,
            my_tile,
        )
        prior = share_priors(local_prior, owned_mask)
        mixing = batch_mixing(prior, obs_values, observation_variance, localization, batch_index)
        sample_vectors_prior = apply_update(sample_vectors_prior, mixing)
    return sample_vectors_prior


def solution(mesh):
    placed = (
        P("mem", None, "dom", None),
        P(None, "dom", None),
        P(),
        P(),
        P(),
        P(),
        P(),
        P(),
        P(),
        P(None, "dom", None),
    )
    return jax.shard_map(
        on_device,
        mesh=mesh,
        in_specs=placed,
        out_specs=P("mem", None, "dom", None),
        check_vma=False,
    )
```

profile of v0, /device:TPU:0, one launch (start us, length us, event | category | flops | bytes accessed | tf_op | source)
XLA Modules:
  0.0 404.2 jit_solution(9559365138855716027)
XLA Ops:
  6.5 1.5 copy.48
  8.1 1.3 collective-permute-start
  9.4 3.0 collective-permute-start.1
  12.4 1.0 copy.41
  13.4 0.5 select_maximum_fusion.2
  14.0 1.4 fusion.4
  15.3 1.3 collective-permute-start.2
  16.6 3.8 collective-permute-start.3
  20.5 0.8 collective-permute-done.3
  21.3 0.5 select_maximum_fusion
  21.8 0.0 copy-start.3
  21.8 0.0 copy-start.10
  21.8 1.4 fusion.3
  23.2 0.0 copy-start.4
  23.2 0.0 copy-start.7
  23.2 0.2 copy.50
  23.4 1.2 reshape.217
  24.6 0.0 all-gather.7.cloned.1.call-update
  24.6 0.0 all-gather.9.cloned.1.call-start
  24.7 0.1 compare_reduce_fusion
  24.8 0.1 broadcast_remainder_fusion
  24.9 0.6 broadcast_add_fusion
  25.5 0.6 add.178
  26.2 0.4 copy.52
  26.6 0.1 compare_reduce_fusion.1
  26.7 0.4 copy.59
  27.1 10.0 %copy.51 = f32[4,40960]{0,1:T(8,128)} copy(f32[4,40960]{1,0:T(4,128)S(1)} %bitcast.60) | data formatting | bytes 1310720 | tf_op jit(solution)/shard_map/reshape | solution.py:90
  37.1 35.3 %gather_fusion = f32[8192,4]{1,0:T(8,128)} fusion(f32[4,40960]{0,1:T(8,128)} %copy.51, s32[8192]{0:T(1024)S(1)} %fusion.31), kind=kCustom, calls=%fused_computation.clone | custom fusion | bytes 294912 | tf_op jit(solution)/shard_map/jit(_take)/gather | solution.py:55
  72.4 6.2 %broadcast_select_fusion.1 = f32[8192,4]{1,0:T(8,128)S(1)} fusion(f32[8192,4]{1,0:T(8,128)} %gather_fusion, pred[8192]{0:T(1024)(128)(4,1)S(1)} %compare_and_fusion.1), kind=kLoop, calls=%fused_computation.11 | loop fusion | flops 32768 | bytes 270336 | tf_op jit(solution)/shard_map/jit(_take)/select_n | solution.py:55
  78.6 11.2 %multiply_reduce_fusion.1 = f32[4,2048]{0,1:T(8,128)S(1)} fusion(f32[4,2048,4]{0,2,1:T(4,128)S(1)} %bitcast.56, f32[2048,4]{1,0:T(8,128)S(1)} %copy.52), kind=kLoop, calls=%fused_computation.7 | loop fusion | flops 57344 | bytes 196608 | tf_op jit(solution)/shard_map/reduce_sum | solution.py:56
  89.8 0.3 broadcast_select_fusion.3
  90.2 72.1 %psum.14 = f32[4,2048]{0,1:T(8,128)} all-reduce(f32[4,2048]{0,1:T(8,128)S(1)} %broadcast_select_fusion.3), channel_id=1, replica_groups=mesh['mem'=8,'dom'=16] {'dom'}, use_global_device_ids=true, to_apply=%region_1.3 | all-reduce | flops 8192 | bytes 65536 | tf_op jit(solution)/shard_map/psum | solution.py:63
  162.3 1.6 copy.53
  163.9 35.0 %all-gather = f32[8,4,2048]{2,1,0:T(4,128)S(1)} all-gather(f32[1,4,2048]{2,1,0:T(4,128)S(1)} %copy.53), channel_id=1, replica_groups=mesh['mem'=8,'dom'=16] {'mem'}, dimensions={0}, use_global_device_ids=true | all-gather | bytes 294912 | tf_op jit(solution)/shard_map/all_gather | solution.py:64
  198.8 0.1 reshape.216
  198.9 0.1 reduce_sum.91
  199.1 0.1 subtract_divide_fusion.1
  199.2 0.4 fusion.17
  199.5 0.1 fusion.41
  199.7 0.0 all-gather.7.cloned.1.call-done
  199.7 3.5 reduce_sum.94
  203.2 6.0 %reshape.218 = f32[32,40960]{1,0:T(8,128)} reshape(f32[8,4,40960]{2,1,0:T(4,128)} %all-gather.7.cloned.1.call-done) | data formatting | bytes 10485760
  209.2 6.0 %fusion.1 = f32[4,40960]{1,0:T(4,128)} fusion(f32[4,40960]{1,0:T(4,128)S(1)} %bitcast.61, f32[32,40960]{1,0:T(8,128)} %reshape.218, f32[40960]{0:T(1024)S(1)} %broadcast_multiply_fusion.1, f32[4]{0:T(128)S(1)} %fusion.41, f32[32,32]{0,1:T(8,128)S(1)} %fusion.17, s32[]{:T(128)S(6)} %select_n.56), kind=kOutput, calls=%fused_computation.5 | convolution fusion | flops 63406208 | bytes 6720004 | tf_op jit(solution)/shard_map/dot_general | solution.py:95
  215.2 0.0 all-gather.9.cloned.1.call-update
  215.2 0.6 add.189
  215.8 0.4 copy.56
  216.2 11.0 %copy.55 = f32[4,40960]{0,1:T(8,128)} copy(f32[4,40960]{1,0:T(4,128)} %fusion.1) | data formatting | bytes 1310720 | tf_op jit(solution)/shard_map/sub | solution.py:100
  227.2 34.7 %gather_fusion.1 = f32[8192,4]{1,0:T(8,128)} fusion(f32[4,40960]{0,1:T(8,128)} %copy.55, s32[8192]{0:T(1024)S(1)} %fusion.32), kind=kCustom, calls=%fused_computation.1.clone | custom fusion | bytes 294912 | tf_op jit(solution)/shard_map/jit(_take)/gather | solution.py:55
  261.9 6.2 %broadcast_select_fusion = f32[8192,4]{1,0:T(8,128)S(1)} fusion(f32[8192,4]{1,0:T(8,128)} %gather_fusion.1, pred[8192]{0:T(1024)(128)(4,1)S(1)} %compare_and_fusion), kind=kLoop, calls=%fused_computation.10 | loop fusion | flops 32768 | bytes 270336 | tf_op jit(solution)/shard_map/jit(_take)/select_n | solution.py:55
  268.2 11.2 %multiply_reduce_fusion = f32[4,2048]{0,1:T(8,128)S(1)} fusion(f32[4,2048,4]{0,2,1:T(4,128)S(1)} %bitcast.57, f32[2048,4]{1,0:T(8,128)S(1)} %copy.56), kind=kLoop, calls=%fused_computation.6 | loop fusion | flops 57344 | bytes 196608 | tf_op jit(solution)/shard_map/reduce_sum | solution.py:56
  279.4 0.3 broadcast_select_fusion.2
  279.7 66.1 %psum.15 = f32[4,2048]{0,1:T(8,128)S(1)} all-reduce(f32[4,2048]{0,1:T(8,128)S(1)} %broadcast_select_fusion.2), channel_id=1, replica_groups=mesh['mem'=8,'dom'=16] {'dom'}, use_global_device_ids=true, to_apply=%region_7.9 | all-reduce | flops 8192 | bytes 65536 | tf_op jit(solution)/shard_map/psum | solution.py:63
  345.9 0.3 copy.57
  346.2 34.7 %all-gather.2 = f32[8,4,2048]{2,1,0:T(4,128)S(1)} all-gather(f32[1,4,2048]{2,1,0:T(4,128)S(1)} %copy.57), channel_id=1, replica_groups=mesh['mem'=8,'dom'=16] {'mem'}, dimensions={0}, use_global_device_ids=true | all-gather | bytes 294912 | tf_op jit(solution)/shard_map/all_gather | solution.py:64
  380.9 0.1 reshape.220
  381.0 0.1 reduce_sum.96
  381.1 0.1 subtract_divide_fusion
  381.2 0.4 fusion.13
  381.6 0.1 fusion.42
  381.7 0.0 all-gather.9.cloned.1.call-done
  381.7 3.5 reduce_sum.99
  385.2 6.1 %reshape.222 = f32[32,40960]{1,0:T(8,128)} reshape(f32[8,4,40960]{2,1,0:T(4,128)} %all-gather.9.cloned.1.call-done) | data formatting | bytes 10485760
  391.3 5.1 %fusion = f32[4,40960]{1,0:T(4,128)S(1)} fusion(f32[4,40960]{1,0:T(4,128)S(1)} %copy-done.2, f32[32,40960]{1,0:T(8,128)} %reshape.222, f32[40960]{0:T(1024)S(1)} %broadcast_multiply_fusion, f32[4]{0:T(128)S(1)} %fusion.42, f32[32,32]{0,1:T(8,128)S(1)} %fusion.13, s32[]{:T(128)S(6)} %select_n.56), kind=kOutput, calls=%fused_computation.3 | convolution fusion | flops 63406208 | bytes 6720004 | tf_op jit(solution)/shard_map/dot_general | solution.py:95
  396.4 1.0 copy.60
  (40 shorter events, 0.3 us)
Async XLA Ops:
  6.5 7.4 %copy-start = (f32[5,5]{1,0:T(8,128)S(1)}, f32[5,5]{1,0:T(8,128)}, u32[]{:S(2)}) copy-start(f32[5,5]{1,0:T(8,128)} %param.16) | copy-start | bytes 304
  6.5 193.1 %all-gather.7.cloned.1.call-start = ((), (), s32[]{:S(2)}) async-start(), calls=%async_computation | async-start | bytes 5898240 | tf_op jit(solution)/shard_map/all_gather | solution.py:94
  8.1 5.4 %collective-permute-start = (f32[4,5,1,256]{3,1,2,0:T(8,128)S(1)}, f32[4,5,1,256]{3,1,2,0:T(8,128)S(1)}, u32[]{:S(2)}, u32[]{:S(2)}) collective-permute-start(f32[4,5,1,256]{3,1,2,0:T(8,128)S(1)} %get-tuple-element.13), channel_id=1, source_target_pairs={{1,0},{2,1},{3,2},{4,3},{5,4},{6,5},{7,6},{8,7},{9,8},{10,9},{11,1... | collective-permute-start | bytes 61448 | tf_op jit(solution)/shard_map/ppermute | solution.py:19
  9.4 4.1 %collective-permute-start.1 = (f32[4,5,1,256]{3,1,2,0:T(8,128)S(1)}, f32[4,5,1,256]{3,1,2,0:T(8,128)S(1)}, u32[]{:S(2)}, u32[]{:S(2)}) collective-permute-start(f32[4,5,1,256]{3,1,2,0:T(8,128)S(1)} %get-tuple-element.12), channel_id=1, source_target_pairs={{0,1},{1,2},{2,3},{3,4},{4,5},{5,6},{6,7},{7,8},{8,9},{9,10},{10,1... | collective-permute-start | bytes 61448 | tf_op jit(solution)/shard_map/ppermute | solution.py:17
  15.3 5.1 %collective-permute-start.2 = (f32[4,5,1,256]{3,1,2,0:T(8,128)S(1)}, f32[4,5,1,256]{3,1,2,0:T(8,128)S(1)}, u32[]{:S(2)}, u32[]{:S(2)}) collective-permute-start(f32[4,5,1,256]{3,1,2,0:T(8,128)S(1)} %get-tuple-element.11), channel_id=1, source_target_pairs={{1,0},{2,1},{3,2},{4,3},{5,4},{6,5},{7,6},{8,7},{9,8},{10,9},{11,1... | collective-permute-start | bytes 61448 | tf_op jit(solution)/shard_map/ppermute | solution.py:19
  16.6 4.7 %collective-permute-start.3 = (f32[4,5,1,256]{3,1,2,0:T(8,128)S(1)}, f32[4,5,1,256]{3,1,2,0:T(8,128)S(1)}, u32[]{:S(2)}, u32[]{:S(2)}) collective-permute-start(f32[4,5,1,256]{3,1,2,0:T(8,128)S(1)} %get-tuple-element.10), channel_id=1, source_target_pairs={{0,1},{1,2},{2,3},{3,4},{4,5},{5,6},{6,7},{7,8},{8,9},{9,10},{10,1... | collective-permute-start | bytes 61448 | tf_op jit(solution)/shard_map/ppermute | solution.py:17
  21.8 2.9 copy-start.3
  21.8 3.0 copy-start.5
  21.8 3.1 copy-start.10
  23.2 3.0 copy-start.4
  23.2 3.3 copy-start.6
  23.2 3.4 copy-start.7
  24.6 357.1 %all-gather.9.cloned.1.call-start = ((), (), s32[]{:S(2)}) async-start(), calls=%async_computation.1 | async-start | bytes 5898240 | tf_op jit(solution)/shard_map/all_gather | solution.py:94
  89.8 109.3 %copy-start.8 = (f32[2,2048]{1,0:T(2,128)S(1)}, f32[2,2048]{1,0:T(2,128)}, u32[]{:S(2)}) copy-start(f32[2,2048]{1,0:T(2,128)} %param.21) | copy-start | bytes 49156
  89.8 109.3 %copy-start.9 = (f32[2,2048]{1,0:T(2,128)S(1)}, f32[2,2048]{1,0:T(2,128)}, u32[]{:S(2)}) copy-start(f32[2,2048]{1,0:T(2,128)} %param.22) | copy-start | bytes 49156
  385.2 6.1 %copy-start.2 = (f32[4,40960]{1,0:T(4,128)S(1)}, f32[4,40960]{1,0:T(4,128)}, u32[]{:S(2)}) copy-start(f32[4,40960]{1,0:T(4,128)} %fusion.1) | copy-start | bytes 1966084
  385.2 12.2 %copy-start.1 = (f32[5,5]{1,0:T(8,128)S(1)}, f32[5,5]{1,0:T(8,128)}, u32[]{:S(2)}) copy-start(f32[5,5]{1,0:T(8,128)} %param.16) | copy-start | bytes 304
Sparse Core Ops, SparseCore 0:
  24.8 87.9 all-gather.6
  215.3 78.2 all-gather.8
where the time goes:
time: 405 us; the launch traced here: 404 us
  blocking collectives  208 us (51%)
  local copies, waits for them, and re-layouts  113 us (28%)
  other arithmetic  44.9 us (11%)
  matrix products  14.5 us (4%)
  between operations  13.9 us (3%)
  starting transfers between devices  9.47 us (2%)
    psum x2, blocking collectives, share_priors(): summed = lax.psum(masked, 'dom')  138 us
    gather x2, local copies, waits for them, and re-layouts, local_priors(): jnp.take(flat, points, axis=1).reshape(sample_total_size, nobs_count, 4)  70 us
    all_gather x2, blocking collectives, share_priors(): prior = lax.all_gather(summed, 'mem', axis=0, tiled=True)  69.7 us
    reduce_sum x2, other arithmetic, local_priors(): local_prior = jnp.sum(values * obs_weights[batch_index][None], axis=-1)  22.4 us
    unnamed x33, local copies, waits for them, and re-layouts  19.3 us
    select_n x2, other arithmetic, local_priors(): jnp.take(flat, points, axis=1).reshape(sample_total_size, nobs_count, 4)  12.4 us
    dot_general x2, matrix products, apply_update(): jnp.dot(own_columns.T, piece, precision=lax.Precision.HIGHEST, preferred_...  11.1 us
    sub x1, local copies, waits for them, and re-layouts, apply_update(): flat + product - jnp.sum(own_columns, axis=0)[:, None] * average[None]  11 us
  transfers between devices with their start and end apart: 6, of which 1 were waited for; matrix products, arithmetic and copies ran while one was open for 33% of the time, Pallas kernels for 0%

commit v1 on v0

--- a/solution.py
+++ b/solution.py
@@ -60,7 +60,7 @@
 
 def share_priors(local_prior, owned_mask):
     masked = jnp.where(owned_mask[None], local_prior, jnp.float32(0.0))
-    summed = lax.psum(masked, "dom")
+    summed = jnp.sum(lax.all_gather(masked, "dom"), axis=0)
     prior = lax.all_gather(summed, "mem", axis=0, tiled=True)
     return prior
 

time: 405 us -> 311 us (0.77)
  blocking collectives: 208 us -> 115 us
    psum x2 -> x0, blocking collectives: 138 us -> none  [share_priors(): summed = lax.psum(masked, 'dom')]
    all_gather x0 -> x2, blocking collectives: none -> 45.7 us  [share_priors(): summed = jnp.sum(lax.all_gather(masked, 'dom'), axis=0)]
    unnamed x33 -> x31, local copies, waits for them, and re-layouts: 19.3 us -> 17.4 us
  transfers between devices with their start and end apart: 6 -> 6, of which waited for: 1 -> 1; matrix products, arithmetic and copies ran while one was open for 33% -> 43% of each run, Pallas kernels for 0% -> 0%
where the time goes in v1:
time: 311 us; the launch traced here: 310 us
  blocking collectives  115 us (37%)
  local copies, waits for them, and re-layouts  111 us (36%)
  other arithmetic  45.1 us (15%)
  matrix products  14.5 us (5%)
  between operations  13.9 us (4%)
  starting transfers between devices  9.47 us (3%)
    gather x2, local copies, waits for them, and re-layouts, local_priors(): jnp.take(flat, points, axis=1).reshape(sample_total_size, nobs_count, 4)  70 us
    all_gather x2, blocking collectives, share_priors(): prior = lax.all_gather(summed, 'mem', axis=0, tiled=True)  69.5 us
    all_gather x2, blocking collectives, share_priors(): summed = jnp.sum(lax.all_gather(masked, 'dom'), axis=0)  45.7 us
    reduce_sum x2, other arithmetic, local_priors(): local_prior = jnp.sum(values * obs_weights[batch_index][None], axis=-1)  22.4 us
    unnamed x31, local copies, waits for them, and re-layouts  17.4 us
    select_n x2, other arithmetic, local_priors(): jnp.take(flat, points, axis=1).reshape(sample_total_size, nobs_count, 4)  12.4 us
    dot_general x2, matrix products, apply_update(): jnp.dot(own_columns.T, piece, precision=lax.Precision.HIGHEST, preferred_...  11.1 us
    sub x1, local copies, waits for them, and re-layouts, apply_update(): flat + product - jnp.sum(own_columns, axis=0)[:, None] * average[None]  11 us
  transfers between devices with their start and end apart: 6, of which 1 were waited for; matrix products, arithmetic and copies ran while one was open for 43% of the time, Pallas kernels for 0%

profile of v1, /device:TPU:0, one launch (start us, length us, event | category | flops | bytes accessed | tf_op | source)
XLA Modules:
  0.0 310.4 jit_solution(10799491245082273566)
XLA Ops:
  6.5 1.5 copy.48
  8.1 1.3 collective-permute-start
  9.4 3.0 collective-permute-start.1
  12.4 1.0 copy.41
  13.4 0.5 select_maximum_fusion.2
  14.0 1.4 fusion.4
  15.3 1.3 collective-permute-start.2
  16.6 3.8 %collective-permute-start.3 = (f32[4,5,1,256]{3,1,2,0:T(8,128)S(1)}, f32[4,5,1,256]{3,1,2,0:T(8,128)S(1)}, u32[]{:S(2)}, u32[]{:S(2)}) collective-permute-start(f32[4,5,1,256]{3,1,2,0:T(8,128)S(1)} %get-tuple-element.10), channel_id=1, source_target_pairs={{0,1},{1,2},{2,3},{3,4},{4,5},{5,6},{6,7},{7,8},{8,9},{9,10},{10,1... | collective-permute-start | bytes 61448 | tf_op jit(solution)/shard_map/ppermute | solution.py:17
  20.5 0.8 collective-permute-done.3
  21.3 0.5 select_maximum_fusion
  21.8 0.0 copy-start.3
  21.8 0.0 copy-start.10
  21.8 1.4 fusion.3
  23.2 0.2 copy.50
  23.4 1.2 reshape.273
  24.6 0.0 all-gather.7.cloned.1.call-update
  24.6 0.0 all-gather.9.cloned.1.call-start
  24.7 0.1 compare_reduce_fusion
  24.8 0.1 broadcast_remainder_fusion
  24.9 0.6 broadcast_add_fusion
  25.5 0.6 add.174
  26.2 0.4 copy.52
  26.6 0.1 compare_reduce_fusion.1
  26.7 0.4 copy.59
  27.1 10.0 %copy.51 = f32[4,40960]{0,1:T(8,128)} copy(f32[4,40960]{1,0:T(4,128)S(1)} %bitcast.64) | data formatting | bytes 1310720 | tf_op jit(solution)/shard_map/reshape | solution.py:90
  37.1 35.3 %gather_fusion = f32[8192,4]{1,0:T(8,128)} fusion(f32[4,40960]{0,1:T(8,128)} %copy.51, s32[8192]{0:T(1024)S(1)} %fusion.31), kind=kCustom, calls=%fused_computation.clone | custom fusion | bytes 294912 | tf_op jit(solution)/shard_map/jit(_take)/gather | solution.py:55
  72.4 6.2 %broadcast_select_fusion.1 = f32[8192,4]{1,0:T(8,128)S(1)} fusion(f32[8192,4]{1,0:T(8,128)} %gather_fusion, pred[8192]{0:T(1024)(128)(4,1)S(1)} %compare_and_fusion.1), kind=kLoop, calls=%fused_computation.11 | loop fusion | flops 32768 | bytes 270336 | tf_op jit(solution)/shard_map/jit(_take)/select_n | solution.py:55
  78.6 11.2 %multiply_reduce_fusion.1 = f32[4,2048]{0,1:T(8,128)S(1)} fusion(f32[4,2048,4]{0,2,1:T(4,128)S(1)} %bitcast.60, f32[2048,4]{1,0:T(8,128)S(1)} %copy.52), kind=kLoop, calls=%fused_computation.7 | loop fusion | flops 57344 | bytes 196608 | tf_op jit(solution)/shard_map/reduce_sum | solution.py:56
  89.8 0.3 bitcast_select_fusion.1
  90.2 0.3 copy.53
  90.5 26.8 %all_gather.20 = f32[16,4,2048]{2,1,0:T(4,128)S(1)} all-gather(f32[1,4,2048]{2,1,0:T(4,128)S(1)} %copy.53), channel_id=1, replica_groups=mesh['mem'=8,'dom'=16] {'dom'}, dimensions={0}, use_global_device_ids=true | all-gather | bytes 557056 | tf_op jit(solution)/shard_map/all_gather | solution.py:63
  117.3 0.1 reduce_sum.114
  117.4 34.9 %all-gather = f32[8,4,2048]{2,1,0:T(4,128)S(1)} all-gather(f32[1,4,2048]{2,1,0:T(4,128)S(1)} %bitcast.67), channel_id=1, replica_groups=mesh['mem'=8,'dom'=16] {'mem'}, dimensions={0}, use_global_device_ids=true | all-gather | bytes 294912 | tf_op jit(solution)/shard_map/all_gather | solution.py:64
  152.2 0.1 reshape.272
  152.3 0.1 reduce_sum.115
  152.5 0.1 subtract_divide_fusion.1
  152.5 0.4 fusion.17
  152.9 0.1 fusion.41
  153.0 0.0 all-gather.7.cloned.1.call-done
  153.1 3.5 %reduce_sum.118 = f32[40960]{0:T(1024)S(1)} reduce(f32[8,4,40960]{2,1,0:T(4,128)} %all-gather.7.cloned.1.call-done, f32[]{:T(128)} %constant.60.clone.1), dimensions={0,1}, to_apply=%region_5.7 | reduce | flops 1269760 | bytes 5406724 | tf_op jit(solution)/shard_map/reduce_sum | solution.py:98
  156.5 6.0 %reshape.274 = f32[32,40960]{1,0:T(8,128)} reshape(f32[8,4,40960]{2,1,0:T(4,128)} %all-gather.7.cloned.1.call-done) | data formatting | bytes 10485760
  162.6 6.0 %fusion.1 = f32[4,40960]{1,0:T(4,128)} fusion(f32[4,40960]{1,0:T(4,128)S(1)} %bitcast.65, f32[32,40960]{1,0:T(8,128)} %reshape.274, f32[40960]{0:T(1024)S(1)} %broadcast_multiply_fusion.1, f32[4]{0:T(128)S(1)} %fusion.41, f32[32,32]{0,1:T(8,128)S(1)} %fusion.17, s32[]{:T(128)S(6)} %select_n.70), kind=kOutput, calls=%fused_computation.5 | convolution fusion | flops 63406208 | bytes 6720004 | tf_op jit(solution)/shard_map/dot_general | solution.py:95
  168.5 0.0 all-gather.9.cloned.1.call-update
  168.6 0.6 add.185
  169.2 0.4 copy.56
  169.6 11.0 %copy.55 = f32[4,40960]{0,1:T(8,128)} copy(f32[4,40960]{1,0:T(4,128)} %fusion.1) | data formatting | bytes 1310720 | tf_op jit(solution)/shard_map/sub | solution.py:100
  180.6 34.7 %gather_fusion.1 = f32[8192,4]{1,0:T(8,128)} fusion(f32[4,40960]{0,1:T(8,128)} %copy.55, s32[8192]{0:T(1024)S(1)} %fusion.32), kind=kCustom, calls=%fused_computation.1.clone | custom fusion | bytes 294912 | tf_op jit(solution)/shard_map/jit(_take)/gather | solution.py:55
  215.3 6.2 %broadcast_select_fusion = f32[8192,4]{1,0:T(8,128)S(1)} fusion(f32[8192,4]{1,0:T(8,128)} %gather_fusion.1, pred[8192]{0:T(1024)(128)(4,1)S(1)} %compare_and_fusion), kind=kLoop, calls=%fused_computation.10 | loop fusion | flops 32768 | bytes 270336 | tf_op jit(solution)/shard_map/jit(_take)/select_n | solution.py:55
  221.5 11.2 %multiply_reduce_fusion = f32[4,2048]{0,1:T(8,128)S(1)} fusion(f32[4,2048,4]{0,2,1:T(4,128)S(1)} %bitcast.61, f32[2048,4]{1,0:T(8,128)S(1)} %copy.56), kind=kLoop, calls=%fused_computation.6 | loop fusion | flops 57344 | bytes 196608 | tf_op jit(solution)/shard_map/reduce_sum | solution.py:56
  232.8 0.3 bitcast_select_fusion
  233.1 0.3 copy.57
  233.4 18.9 %all_gather.23 = f32[16,4,2048]{2,1,0:T(4,128)S(1)} all-gather(f32[1,4,2048]{2,1,0:T(4,128)S(1)} %copy.57), channel_id=1, replica_groups=mesh['mem'=8,'dom'=16] {'dom'}, dimensions={0}, use_global_device_ids=true | all-gather | bytes 557056 | tf_op jit(solution)/shard_map/all_gather | solution.py:63
  252.4 0.1 reduce_sum.121
  252.5 34.6 %all-gather.2 = f32[8,4,2048]{2,1,0:T(4,128)S(1)} all-gather(f32[1,4,2048]{2,1,0:T(4,128)S(1)} %bitcast.68), channel_id=1, replica_groups=mesh['mem'=8,'dom'=16] {'mem'}, dimensions={0}, use_global_device_ids=true | all-gather | bytes 294912 | tf_op jit(solution)/shard_map/all_gather | solution.py:64
  287.1 0.1 reshape.276
  287.2 0.1 reduce_sum.122
  287.3 0.1 subtract_divide_fusion
  287.4 0.4 fusion.13
  287.8 0.1 fusion.42
  287.9 0.0 all-gather.9.cloned.1.call-done
  287.9 3.5 %reduce_sum.125 = f32[40960]{0:T(1024)S(1)} reduce(f32[8,4,40960]{2,1,0:T(4,128)} %all-gather.9.cloned.1.call-done, f32[]{:T(128)} %constant.60.clone.1), dimensions={0,1}, to_apply=%region_11.13 | reduce | flops 1269760 | bytes 5406724 | tf_op jit(solution)/shard_map/reduce_sum | solution.py:98
  291.4 6.1 %reshape.278 = f32[32,40960]{1,0:T(8,128)} reshape(f32[8,4,40960]{2,1,0:T(4,128)} %all-gather.9.cloned.1.call-done) | data formatting | bytes 10485760
  297.5 5.1 %fusion = f32[4,40960]{1,0:T(4,128)S(1)} fusion(f32[4,40960]{1,0:T(4,128)S(1)} %copy-done.2, f32[32,40960]{1,0:T(8,128)} %reshape.278, f32[40960]{0:T(1024)S(1)} %broadcast_multiply_fusion, f32[4]{0:T(128)S(1)} %fusion.42, f32[32,32]{0,1:T(8,128)S(1)} %fusion.13, s32[]{:T(128)S(6)} %select_n.70), kind=kOutput, calls=%fused_computation.3 | convolution fusion | flops 63406208 | bytes 6720004 | tf_op jit(solution)/shard_map/dot_general | solution.py:95
  302.6 1.0 copy.60
  (42 shorter events, 0.3 us)
Async XLA Ops:
  6.5 7.4 %copy-start = (f32[5,5]{1,0:T(8,128)S(1)}, f32[5,5]{1,0:T(8,128)}, u32[]{:S(2)}) copy-start(f32[5,5]{1,0:T(8,128)} %param.16) | copy-start | bytes 304
  6.5 146.5 %all-gather.7.cloned.1.call-start = ((), (), s32[]{:S(2)}) async-start(), calls=%async_computation | async-start | bytes 5898240 | tf_op jit(solution)/shard_map/all_gather | solution.py:94
  8.1 5.4 %collective-permute-start = (f32[4,5,1,256]{3,1,2,0:T(8,128)S(1)}, f32[4,5,1,256]{3,1,2,0:T(8,128)S(1)}, u32[]{:S(2)}, u32[]{:S(2)}) collective-permute-start(f32[4,5,1,256]{3,1,2,0:T(8,128)S(1)} %get-tuple-element.13), channel_id=1, source_target_pairs={{1,0},{2,1},{3,2},{4,3},{5,4},{6,5},{7,6},{8,7},{9,8},{10,9},{11,1... | collective-permute-start | bytes 61448 | tf_op jit(solution)/shard_map/ppermute | solution.py:19
  9.4 4.1 %collective-permute-start.1 = (f32[4,5,1,256]{3,1,2,0:T(8,128)S(1)}, f32[4,5,1,256]{3,1,2,0:T(8,128)S(1)}, u32[]{:S(2)}, u32[]{:S(2)}) collective-permute-start(f32[4,5,1,256]{3,1,2,0:T(8,128)S(1)} %get-tuple-element.12), channel_id=1, source_target_pairs={{0,1},{1,2},{2,3},{3,4},{4,5},{5,6},{6,7},{7,8},{8,9},{9,10},{10,1... | collective-permute-start | bytes 61448 | tf_op jit(solution)/shard_map/ppermute | solution.py:17
  15.3 5.1 %collective-permute-start.2 = (f32[4,5,1,256]{3,1,2,0:T(8,128)S(1)}, f32[4,5,1,256]{3,1,2,0:T(8,128)S(1)}, u32[]{:S(2)}, u32[]{:S(2)}) collective-permute-start(f32[4,5,1,256]{3,1,2,0:T(8,128)S(1)} %get-tuple-element.11), channel_id=1, source_target_pairs={{1,0},{2,1},{3,2},{4,3},{5,4},{6,5},{7,6},{8,7},{9,8},{10,9},{11,1... | collective-permute-start | bytes 61448 | tf_op jit(solution)/shard_map/ppermute | solution.py:19
  16.6 4.7 %collective-permute-start.3 = (f32[4,5,1,256]{3,1,2,0:T(8,128)S(1)}, f32[4,5,1,256]{3,1,2,0:T(8,128)S(1)}, u32[]{:S(2)}, u32[]{:S(2)}) collective-permute-start(f32[4,5,1,256]{3,1,2,0:T(8,128)S(1)} %get-tuple-element.10), channel_id=1, source_target_pairs={{0,1},{1,2},{2,3},{3,4},{4,5},{5,6},{6,7},{7,8},{8,9},{9,10},{10,1... | collective-permute-start | bytes 61448 | tf_op jit(solution)/shard_map/ppermute | solution.py:17
  21.8 2.9 copy-start.3
  21.8 3.0 copy-start.5
  21.8 3.1 copy-start.10
  23.2 3.0 copy-start.4
  23.2 3.3 %copy-start.6 = (s32[2,2048,1]{1,2,0:T(1,128)S(1)}, s32[2,2048,1]{1,2,0:T(1,128)}, u32[]{:S(2)}) copy-start(s32[2,2048,1]{1,2,0:T(1,128)} %param.17) | copy-start | bytes 49156
  23.2 3.4 %copy-start.7 = (f32[2,1,2048]{2,1,0:T(1,128)S(1)}, f32[2,1,2048]{2,1,0:T(1,128)}, u32[]{:S(2)}) copy-start(f32[2,1,2048]{2,1,0:T(1,128)} %param.23) | copy-start | bytes 49156
  24.6 263.3 %all-gather.9.cloned.1.call-start = ((), (), s32[]{:S(2)}) async-start(), calls=%async_computation.1 | async-start | bytes 5898240 | tf_op jit(solution)/shard_map/all_gather | solution.py:94
  89.8 62.6 %copy-start.8 = (f32[2,2048]{1,0:T(2,128)S(1)}, f32[2,2048]{1,0:T(2,128)}, u32[]{:S(2)}) copy-start(f32[2,2048]{1,0:T(2,128)} %param.21) | copy-start | bytes 49156
  89.8 62.6 %copy-start.9 = (f32[2,2048]{1,0:T(2,128)S(1)}, f32[2,2048]{1,0:T(2,128)}, u32[]{:S(2)}) copy-start(f32[2,2048]{1,0:T(2,128)} %param.22) | copy-start | bytes 49156
  291.4 6.1 %copy-start.2 = (f32[4,40960]{1,0:T(4,128)S(1)}, f32[4,40960]{1,0:T(4,128)}, u32[]{:S(2)}) copy-start(f32[4,40960]{1,0:T(4,128)} %fusion.1) | copy-start | bytes 1966084
  291.4 12.2 %copy-start.1 = (f32[5,5]{1,0:T(8,128)S(1)}, f32[5,5]{1,0:T(8,128)}, u32[]{:S(2)}) copy-start(f32[5,5]{1,0:T(8,128)} %param.16) | copy-start | bytes 304
Sparse Core Ops, SparseCore 0:
  24.8 87.9 all-gather.6
  168.7 78.3 all-gather.8
